TPU v7x, 32 devices: a whole 2x2x4 slice. The times are simulated.
32 devices in a mesh: lat: 8 (over z, y), depth: 4 (over x, core).
Axes of the slice: x: 2, y: 2, z: 4, core: 2. Of those that a mesh axis runs over, the one named last changes fastest.
Arguments:
- grade_field: float32 [64, 128, 2048], P('depth', 'lat'), may hold values from 0 to 1
- amplitude: float32 [64, 128, 2048], P('depth', 'lat'), may hold values from -6 to 6
- tf_table: int32 [4, 128], replicated, may hold values from 0 to 65535
- brick_mask: int32 [8, 16, 8], P('depth', 'lat'), may hold values 0 or 1
Outputs:
- frame: float32 [4, 128, 2048], P(None, 'lat', 'depth')
All inputs are finite; a program needn't handle non-finite values. No bound on the sum of `brick_mask` on one device may be relied on, other than what follows from the above.
Results may differ from a plain program's by a relative error of at most 0.00073.
Values sent between devices are 32-bit elements; how exact they have to be, the bound alone decides.
No kernel may reach another device: no remote copies, remote signals or barrier semaphores. Data moves between devices by JAX's collectives and lax.ppermute only.
A program may use at most 128 MiB of HBM per device.

v0:
```python
import functools

import jax
import jax.numpy as jnp
from jax import lax
from jax.experimental import pallas as pl
from jax.experimental.pallas import tpu as pltpu
from jax.sharding import PartitionSpec as P

MZ = 8
MX = 8
MY = 256
LANES = 128
SUB = 8
TERMS = 9


def sublane(shape):
    return lax.broadcasted_iota(jnp.int32, shape, len(shape) - 2)


PLACES = ((6, 4, 2, 0), (0, 6, 4, 2))


def row_copies(fields, out_ref, sems, last):
    slices, rows = fields[0].shape[:2]
    span = slices // 4
    made = []
    for f, src in enumerate(fields):
        for q in range(4):
            here = src.at[pl.ds(span * q, span), pl.ds(rows - 2 if last else 0, 2), :]
            made.append(pltpu.make_async_copy(here, out_ref.at[f, :, pl.ds(PLACES[last][q], 2), :], sems.at[f, q]))
    return made


def start_and_wait(copies):
    for copy in copies:
        copy.start()
    for copy in copies:
        copy.wait()


def pair_kernel(lat_ref, grade_hbm, amp_hbm, pair_ref, sems):
    odd = lax.rem(lat_ref[0], 2)
    for last in (0, 1):
        @pl.when(odd == 1 - last)
        def _():
            start_and_wait(row_copies((grade_hbm, amp_hbm), pair_ref, sems, last))


def rest_kernel(lat_ref, depth_ref, grade_hbm, amp_hbm, after_ref, cross_ref, near_ref, far_ref, sems, depth_sems):
    del after_ref
    slices = grade_hbm.shape[0]
    fields = (grade_hbm, amp_hbm)
    odd = lax.rem(depth_ref[0], 2)
    parallel = []
    for f, src in enumerate(fields):
        for n, (dst, at) in enumerate(((near_ref, 1 - odd), (far_ref, odd))):
            here = src.at[pl.ds(at * (slices - 2), 2)]
            parallel.append(pltpu.make_async_copy(here, dst.at[f], depth_sems.at[f, n]))
    odd_lat = lax.rem(lat_ref[0], 2)
    for last in (0, 1):
        @pl.when(odd_lat == last)
        def _():
            start_and_wait(row_copies(fields, cross_ref, sems, last) + parallel)


def pass_on_kernel(*refs):
    del refs


def pass_on(x, *earlier):
    spec = pl.BlockSpec(memory_space=pl.ANY)
    return pl.pallas_call(
        pass_on_kernel,
        out_shape=jax.ShapeDtypeStruct(x.shape, x.dtype),
        in_specs=[spec] * (1 + len(earlier)),
        out_specs=spec,
        input_output_aliases={0: 0},
        compiler_params=pltpu.CompilerParams(vmem_limit_bytes=1 << 20),
        name="pass_on",
    )(x, *earlier)


def round_weight(w):
    return w.astype(jnp.bfloat16).astype(jnp.float32)


def stencil(m2, m1, p1, p2):
    return (m2 - p2) + 8.0 * (p1 - m1)


def fill_tables(scale, table_ref, low_ref, high_ref):
    bins = table_ref.shape[1]
    table = (table_ref[...].astype(jnp.float32) / 65535.0).astype(jnp.bfloat16).astype(jnp.float32)
    table = jnp.where(sublane(table.shape) == 3, table * scale, table)
    column = lax.broadcasted_iota(jnp.int32, table.shape, 1)
    following = jnp.where(column == bins - 1, 0.0, pltpu.roll(table, bins - 1, 1))
    for c in range(4):
        low_ref[c] = jnp.broadcast_to(table[c:c + 1, :], (SUB, bins))
        high_ref[c] = jnp.broadcast_to(following[c:c + 1, :], (SUB, bins))


class Field:
    def __init__(self, ref, slices, strips, s):
        self.ref, self.strips = ref, strips
        self.per_slice = ref.shape[0] // slices
        self.s = s

    def load(self, z, rt, ds=0, k=0):
        start = pl.multiple_of((self.s + ds) * SUB, SUB) + (z * self.per_slice + rt * self.strips * SUB + k)
        return self.ref[pl.ds(start, SUB), :]

    def columns(self, z, rt, mid, lane):
        left = jnp.where(self.s > 0, self.load(z, rt, -jnp.minimum(self.s, 1)), 0.0)
        right = jnp.where(self.s < self.strips - 1, self.load(z, rt, jnp.minimum(self.strips - 1 - self.s, 1)), 0.0)
        return stencil(
            pltpu.roll(jnp.where(lane >= LANES - 2, left, mid), 2, 1),
            pltpu.roll(jnp.where(lane >= LANES - 1, left, mid), 1, 1),
            pltpu.roll(jnp.where(lane < 1, right, mid), LANES - 1, 1),
            pltpu.roll(jnp.where(lane < 2, right, mid), LANES - 2, 1),
        )

    def rows(self, z, rt, mid, sub, roll):
        def shifted(k):
            if k > 0:
                inside = sub < SUB - k
                if rt == 0:
                    return jnp.where(inside, self.load(z, 0, 0, k), self.load(z, 1, 0, k - SUB))
                return jnp.where(inside, pltpu.roll(mid, SUB - k, 0) if roll else self.load(z, 1, 0, k), 0.0)
            inside = sub >= -k
            if rt == 1:
                return jnp.where(inside, self.load(z, 1, 0, k), self.load(z, 0, 0, SUB + k))
            return jnp.where(inside, pltpu.roll(mid, -k, 0) if roll else self.load(z, 0, 0, k), 0.0)

        return stencil(*(shifted(k) for k in (-2, -1, 1, 2)))


def classify(grade, bins, low_ref, high_ref):
    position = grade * (bins - 1.0)
    index = jnp.minimum(position.astype(jnp.int32), bins - 1)
    w_low = 1.0 - (position - index.astype(jnp.float32))
    w_high = round_weight(1.0 - w_low)
    w_low = round_weight(w_low)

    def gather(ref, c):
        return jnp.take_along_axis(ref[c], index, axis=1)

    return [w_low * gather(low_ref, c) + w_high * gather(high_ref, c) for c in range(4)]


def step(state, terms):
    red, green, blue, trans = state
    g_x, a_x, g_yz, a_yz, steep, *cls = terms
    edge = 1.0 - 12.0 * lax.rsqrt(a_x * a_x + a_yz)
    shade = 0.3 + steep * lax.rsqrt(g_x * g_x + g_yz)
    weight = trans * (cls[3] * edge)
    trans = trans - weight
    weight = weight * shade
    return (red + weight * cls[0], green + weight * cls[1], blue + weight * cls[2], trans)


def cell_terms(fields, z, rt, along, roll, bins, low_ref, high_ref):
    lane = lax.broadcasted_iota(jnp.int32, (SUB, LANES), 1)
    sub = sublane((SUB, LANES))
    parts = []
    for field, near in zip(fields, along):
        mid = field.load(z, rt)
        dy = field.columns(z, rt, mid, lane)
        dz = stencil(*near)
        parts.append((mid, field.rows(z, rt, mid, sub, roll), dy * dy + dz * dz, dz))
    (grade, g_x, g_yz, g_z), (_, a_x, a_yz, _) = parts
    cls = classify(grade, bins, low_ref, high_ref)
    return (g_x, a_x, g_yz + 36.0, a_yz + 144.0, 0.7 * jnp.abs(g_z), *cls)


KEPT_AT = ((0, 4), (6, 2))


def keep(kept_ref, zi, s, rt, zb, terms):
    rows = slice(0, 2) if rt == 0 else slice(SUB - 2, SUB)
    at = KEPT_AT[rt][zb]
    for n, term in enumerate(terms):
        kept_ref[zi, s, n, at:at + 2, :] = term[rows, :]


BLANK = (0.0, 0.0, 36.0, 144.0, 0.0, 0.0, 0.0, 0.0, 0.0)


def blank(kept_ref, zi, s, rt, zb):
    at = KEPT_AT[rt][zb]
    for n, value in enumerate(BLANK):
        kept_ref[zi, s, n, at:at + 2, :] = jnp.full((2, LANES), value, jnp.float32)


def middle_kernel(scale, slices, strips, mask_ref, grade_ref, amp_ref, table_ref, mid_ref, kept_ref, low_ref, high_ref):
    bins = table_ref.shape[1]
    fill_tables(scale, table_ref, low_ref, high_ref)
    per_block = MY // LANES
    zero = jnp.zeros((SUB, LANES), jnp.float32)

    def block(cb, carry):
        for rt in range(2):
            def march(halves):
                for j in range(per_block):
                    s = cb * per_block + j
                    fields = [Field(ref, slices, strips, s) for ref in (grade_ref, amp_ref)]
                    state = (zero, zero, zero, zero + 1.0)
                    for zb in halves:
                        for zi in range(2 - 2 * zb, MZ - 2 * zb):
                            z = zb * MZ + zi
                            along = [[field.load(z + k, rt) for k in (-2, -1, 1, 2)] for field in fields]
                            terms = cell_terms(fields, z, rt, along, False, bins, low_ref, high_ref)
                            keep(kept_ref, zi, s, rt, zb, terms)
                            state = step(state, terms)
                    for zb in {0, 1} - set(halves):
                        for zi in range(2 - 2 * zb, MZ - 2 * zb):
                            blank(kept_ref, zi, s, rt, zb)
                    for c in range(4):
                        mid_ref[rt, s, c] = state[c]

            front, back = mask_ref[0, rt, cb] != 0, mask_ref[1, rt, cb] != 0
            pl.when(front & back)(functools.partial(march, (0, 1)))
            pl.when(front & ~back)(functools.partial(march, (0,)))
            pl.when(~front & back)(functools.partial(march, (1,)))
            pl.when(~front & ~back)(functools.partial(march, ()))
        return carry

    lax.fori_loop(0, strips // per_block, block, 0)


def ends_kernel(scale, pieces, slices, strips, for_sibling, mask_ref, depth_ref, grade_ref, amp_ref, near_ref, far_ref,
                table_ref, mid_ref, middle_kept_ref, *rest):
    out_ref, kept_ref, acc_ref, low_ref, high_ref = rest[-5:]
    bins = table_ref.shape[1]
    fill_tables(scale, table_ref, low_ref, high_ref)
    per_block = MY // LANES
    piece_strips = strips // pieces
    piece_blocks = piece_strips // per_block
    zero = jnp.zeros((SUB, LANES), jnp.float32)
    odd = jnp.broadcast_to(lax.rem(depth_ref[0], 2), (SUB, LANES)) == 1

    own_bit = lax.rem(depth_ref[0], 2)
    first_piece = 1 - own_bit if for_sibling else own_bit

    def block(n, carry):
        piece = first_piece + 2 * (n // piece_blocks)
        cb = piece * piece_blocks + lax.rem(n, piece_blocks)
        owner = lax.bitwise_xor(piece, depth_ref[0])
        full = [[mask_ref[zb, rt, cb] for rt in range(2)] for zb in range(2)]

        def march():
            for j in range(per_block):
                s = cb * per_block + j
                for n in range(TERMS):
                    for k, zi in enumerate((0, 1, MZ - 2, MZ - 1)):
                        kept_ref[k, s, n] = middle_kept_ref[zi, s, n]
            for rt in range(2):
                for j in range(per_block):
                    s = cb * per_block + j
                    fields = [Field(ref, slices, strips, s) for ref in (grade_ref, amp_ref)]
                    near, far = (Field(ref, 4, strips, s) for ref in (near_ref, far_ref))
                    state = (zero, zero, zero, zero + 1.0)
                    for zb in range(2):
                        cover = jnp.broadcast_to(full[zb][rt], (SUB, LANES)).astype(jnp.float32)
                        if zb == 1:
                            red, green, blue, trans = state
                            state = tuple(
                                value + trans * mid_ref[rt, s, c] for c, value in enumerate((red, green, blue))
                            ) + (trans * mid_ref[rt, s, 3],)
                        for zi in (0, 1) if zb == 0 else (MZ - 2, MZ - 1):
                            z = zb * MZ + zi
                            along = []
                            for f in range(2):

                                def at(z):
                                    if 0 <= z < slices:
                                        return fields[f].load(z, rt)
                                    k = 2 * f + z % slices % 2
                                    one, two = near.load(k, rt), far.load(k, rt)
                                    return jnp.where(odd, one, two) if z < 0 else jnp.where(odd, two, one)

                                along.append([at(z + k) for k in (-2, -1, 1, 2)])
                            terms = cell_terms(fields, z, rt, along, z in (0, slices - 1), bins, low_ref, high_ref)
                            terms = (*terms[:-1], terms[-1] * cover)
                            keep(kept_ref, zi if zb == 0 else zi - 4, s, rt, zb, terms)
                            state = step(state, terms)
                    for c in range(4):
                        acc_ref[rt, j, c] = state[c]

        some = (full[0][0] | full[0][1] | full[1][0] | full[1][1]) != 0
        pl.when(some)(march)

        @pl.when(jnp.logical_not(some))
        def _():
            for j in range(per_block):
                for n, value in enumerate(BLANK):
                    for k in range(4):
                        kept_ref[k, cb * per_block + j, n] = jnp.full((SUB, LANES), value, jnp.float32)
            for rt in range(2):
                for j in range(per_block):
                    for c in range(4):
                        acc_ref[rt, j, c] = zero if c < 3 else zero + 1.0

        for rt in range(2):
            for c in range(4):
                for j in range(per_block):
                    part = lax.rem(cb, piece_blocks) * MY + j * LANES
                    lanes = pl.ds(pl.multiple_of(part, LANES), LANES)
                    out_ref[owner // 2, c, rt * SUB:(rt + 1) * SUB, lanes] = acc_ref[rt, j, c]
        return carry

    lax.fori_loop(0, pieces // 2 * piece_blocks, block, 0)


def edge_kernel(pieces, which, depth_ref, lat_ref, kept_ref, stay_ref, go_ref, pair_ref, cross_ref, after_ref, *outs):
    del after_ref
    half = kept_ref.shape[0]
    strips = kept_ref.shape[1]
    sub = sublane((SUB, LANES))
    is_first = lax.rem((sub + 2) // 4, 2) == 0
    odd_lat = jnp.broadcast_to(lax.rem(lat_ref[0], 2), (SUB, LANES))
    from_pair = lax.rem(sub // 2, 2) != odd_lat
    piece_strips = strips // pieces
    packs = piece_strips // 2

    above = lax.rem(sub // 2, 2) == 0
    even_row = lax.rem(sub, 2) == 0

    own_factor = jnp.where(above, 1.0, -1.0)
    mate_factor = jnp.where(above == even_row, -8.0 * own_factor, 0.0)

    def outside(raw):
        mate = jnp.where(even_row, pltpu.roll(raw, SUB - 1, 0), pltpu.roll(raw, 1, 0))
        return own_factor * raw + mate_factor * mate

    def halo(f, zi, lanes):
        pair, cross = pair_ref[f, zi % 4, :, lanes], cross_ref[f, zi % 4, :, lanes]
        if zi < 4:
            return outside(jnp.where(from_pair, pair, cross))
        return outside(pltpu.roll(jnp.where(from_pair, cross, pair), 2, 0))

    def strip(s, ends_ref):
        lanes = pl.ds(pl.multiple_of(s * LANES, LANES), LANES)
        zero = jnp.zeros((SUB, LANES), jnp.float32)
        state = (zero, zero, zero, zero + 1.0)
        for zi in range(half):
            held, at = (kept_ref, zi) if 2 <= zi < half - 2 else (ends_ref, zi % (half - 4))
            g_x, a_x, *others = (held[at, s, n] for n in range(TERMS))
            state = step(state, (g_x + halo(0, zi, lanes), a_x + halo(1, zi, lanes), *others))
        *total, trans = state
        out = [t + trans * pltpu.roll(t, 4, 0) for t in total]
        return out + [trans * pltpu.roll(trans, 4, 0)]

    for n, out in zip(which, outs):
        p = lax.bitwise_xor(n, depth_ref[0])
        results = [strip(p * piece_strips + j, go_ref if n % 2 else stay_ref) for j in range(piece_strips)]
        for j in range(packs):
            for c, (one, two) in enumerate(zip(results[j], results[j + packs])):
                out[c, :, j * LANES:(j + 1) * LANES] = jnp.where(is_first, one, pltpu.roll(two, 4, 0))


def merge(mine, other, rank, level):
    ahead = jnp.broadcast_to(lax.rem(lax.shift_right_logical(rank, level), 2), mine[3].shape) == 0
    clear = jnp.where(ahead, mine[3], other[3])
    return [
        jnp.where(ahead, m, o) + clear * jnp.where(ahead, o, m) for m, o in zip(mine[:3], other[:3])
    ] + [mine[3] * other[3]]


def channels(ref):
    return [ref[c] for c in range(4)]


def merge_kernel(depth_ref, stay_ref, got_ref, own_ref, away_ref):
    for n, out_ref in enumerate((own_ref, away_ref)):
        for c, value in enumerate(merge(channels(stay_ref.at[n]), channels(got_ref.at[n]), depth_ref[0], 0)):
            out_ref[c] = value


def finish_kernel(depth_ref, own_ref, got_ref, home_ref, across_ref, corner_ref, beside_ref, out_ref):
    rows = out_ref.shape[1]
    rank = depth_ref[0]
    frame = merge(channels(own_ref), channels(got_ref), rank, 1)
    near = merge(channels(home_ref), channels(beside_ref), rank, 0)
    far = merge(channels(across_ref), channels(corner_ref), rank, 0)
    rim = merge(near, far, rank, 1)
    for c in range(4):
        inner, packed = frame[c], rim[c]
        if c == 3:
            inner, packed = 1.0 - inner, 1.0 - packed
        wide = jnp.concatenate([packed, pltpu.roll(packed, 4, 0)], axis=1)
        sub = sublane(wide.shape)
        out_ref[c, 0:SUB, :] = jnp.where(sub < 2, wide, inner[0:SUB, :])
        out_ref[c, rows - SUB:rows, :] = jnp.where(sub >= SUB - 2, wide, inner[rows - SUB:rows, :])


def swap_near(x, axis):
    return lax.ppermute(x, axis, [(i, i ^ 1) for i in range(lax.axis_size(axis))])


def swap_far(x, axis):
    size = lax.axis_size(axis)
    return lax.ppermute(x, axis, [(i, j) for k in range(1, size - 1, 2) for i, j in ((k, k + 1), (k + 1, k))])


def by_strips(array):
    rows, cols = array.shape[-2:]
    split = array.reshape(-1, rows // SUB, SUB, cols // LANES, LANES)
    return split.transpose(0, 1, 3, 2, 4).reshape(-1, LANES)


def local(grade_field, amplitude, tf_table, brick_mask):
    slices, rows, cols = grade_field.shape
    pieces = lax.axis_size("depth")
    assert (slices, rows, pieces) == (2 * MZ, 2 * MX, 4)
    depth_rank = lax.axis_index("depth").astype(jnp.int32).reshape(1)
    lat_rank = lax.axis_index("lat").astype(jnp.int32).reshape(1)
    f32 = jnp.float32
    vmem = pl.BlockSpec(memory_space=pltpu.VMEM)
    smem = pl.BlockSpec(memory_space=pltpu.SMEM)
    hbm = pl.BlockSpec(memory_space=pltpu.MemorySpace.HBM)
    lat_halo = jax.ShapeDtypeStruct((2, slices // 4, SUB, cols), f32)
    depth_halo = jax.ShapeDtypeStruct((2, 2, rows, cols), f32)
    hbm_only = pltpu.MemorySpace.HBM
    fields = (grade_field, amplitude)
    grade_field = pltpu.with_memory_space_constraint(grade_field, hbm_only)
    amplitude = pltpu.with_memory_space_constraint(amplitude, hbm_only)
    small = pltpu.CompilerParams(vmem_limit_bytes=4 << 20)
    after = pl.BlockSpec(memory_space=pl.ANY)
    pair = pl.pallas_call(
        pair_kernel,
        out_shape=lat_halo,
        in_specs=[smem, hbm, hbm],
        out_specs=vmem,
        scratch_shapes=[pltpu.SemaphoreType.DMA((2, 4))],
        compiler_params=small,
        name="take_pair",
    )(lat_rank, grade_field, amplitude)
    cross, near, far = pl.pallas_call(
        rest_kernel,
        out_shape=(lat_halo, depth_halo, depth_halo),
        in_specs=[smem, smem, hbm, hbm, after],
        out_specs=[vmem] * 3,
        scratch_shapes=[pltpu.SemaphoreType.DMA((2, 4)), pltpu.SemaphoreType.DMA((2, 2))],
        compiler_params=small,
        name="take_rest",
    )(lat_rank, depth_rank, grade_field, amplitude, pair)
    far = pass_on(far, cross)
    near = pass_on(near, far)
    pair = swap_near(pair, "lat")
    cross = swap_far(cross, "lat")
    near = swap_near(near, "depth")
    far = swap_far(far, "depth")
    piece = jax.ShapeDtypeStruct((4, rows, cols // pieces), f32)
    half = jax.ShapeDtypeStruct((2, *piece.shape), f32)
    scale = 4.0 / (slices * pieces)
    strips = cols // LANES
    table = pltpu.VMEM((4, SUB, tf_table.shape[1]), f32)
    grade_strips, amp_strips = by_strips(fields[0]), by_strips(fields[1])
    mid, kept = pl.pallas_call(
        functools.partial(middle_kernel, scale, slices, strips),
        out_shape=(
            jax.ShapeDtypeStruct((2, strips, 4, SUB, LANES), f32),
            jax.ShapeDtypeStruct((MZ, strips, TERMS, SUB, LANES), f32),
        ),
        in_specs=[smem, vmem, vmem, vmem],
        out_specs=[vmem, vmem],
        scratch_shapes=[table, table],
        compiler_params=pltpu.CompilerParams(vmem_limit_bytes=8 << 20),
        cost_estimate=pl.CostEstimate(flops=10**10, bytes_accessed=10**8, transcendentals=0),
        name="middle",
    )(brick_mask, grade_strips, amp_strips, tf_table)

    def march_ends(for_sibling, *earlier):
        return pl.pallas_call(
            functools.partial(ends_kernel, scale, pieces, slices, strips, for_sibling),
            out_shape=(half, jax.ShapeDtypeStruct((4, strips, TERMS, SUB, LANES), f32)),
            in_specs=[smem, smem] + [vmem] * 7 + [after] * len(earlier),
            out_specs=[vmem] * 2,
            scratch_shapes=[pltpu.VMEM((2, MY // LANES, 4, SUB, LANES), f32), table, table],
            compiler_params=small,
            name="ends",
        )(brick_mask, depth_rank, grade_strips, amp_strips, by_strips(near), by_strips(far), tf_table, mid, kept, *earlier)

    go, kept_go = march_ends(True)
    stay, kept_stay = march_ends(False, go)

    def swap_across(x):
        return lax.ppermute(x, "depth", [(i, i ^ 2) for i in range(pieces)])

    own, away_inner = pl.pallas_call(
        merge_kernel,
        out_shape=(piece, piece),
        in_specs=[smem, vmem, vmem],
        out_specs=[vmem, vmem],
        compiler_params=small,
        name="merge",
    )(depth_rank, stay, swap_near(go, "depth"))
    got = swap_across(away_inner)
    rim = jax.ShapeDtypeStruct((4, SUB, cols // pieces // 2), f32)

    def edges_of(which, earlier):
        return pl.pallas_call(
            functools.partial(edge_kernel, pieces, which),
            out_shape=(rim,) * len(which),
            in_specs=[smem, smem] + [vmem] * 5 + [after],
            out_specs=[vmem] * len(which),
            compiler_params=small,
            name="edges",
        )(depth_rank, lat_rank, kept, kept_stay, kept_go, pair, cross, earlier)

    across, corner, beside = edges_of((2, 3, 1), away_inner)
    (home,) = edges_of((0,), beside)
    beside = swap_near(beside, "depth")
    across = swap_across(across)
    corner = lax.ppermute(corner, "depth", [(i, i ^ 3) for i in range(pieces)])
    edges = (home, beside, across, corner)
    return pl.pallas_call(
        finish_kernel,
        out_shape=piece,
        in_specs=[smem] + [vmem] * 6,
        out_specs=vmem,
        compiler_params=small,
        name="finish",
    )(depth_rank, own, got, edges[0], edges[2], edges[3], edges[1])


def solution(mesh):
    placed = (P("depth", "lat", None), P("depth", "lat", None), P(), P("depth", "lat", None))
    return jax.shard_map(
        local, mesh=mesh, in_specs=placed, out_specs=P(None, "lat", "depth"), check_vma=False
    )
```

profile of v0, /device:TPU:0, one launch (start us, length us, event | category | flops | bytes accessed | tf_op | source)
XLA Modules:
  0.0 32.7 jit_solution(17147711888977797600)
XLA Ops:
  0.0 1.1 %take_pair.1.after_ref = f32[2,4,8,2048]{3,2,1,0:T(8,128)S(1)} custom-call(s32[1]{0:T(128)} %bitcast.7.lat_ref, f32[16,16,2048]{2,1,0:T(8,128)} %grade_hbm.3, f32[16,16,2048]{2,1,0:T(8,128)} %amp_hbm.3), custom_call_target="tpu_custom_call" | custom-call | tf_op jit(solution)/shard_map/take_pair/pallas_call | solution.py:431
  1.1 3.0 %collective-permute-start.4 = (f32[2,4,8,2048]{3,2,1,0:T(8,128)S(1)}, f32[2,4,8,2048]{3,2,1,0:T(8,128)S(1)}, u32[]{:S(2)}, u32[]{:S(2)}) collective-permute-start(f32[2,4,8,2048]{3,2,1,0:T(8,128)S(1)} %take_pair.1.after_ref), channel_id=1, source_target_pairs={{0,4},{4,0},{8,12},{12,8},{16,20},{20,16},{24,28},{28,24},{1,5},{5... | collective-permute-start | bytes 1572872 | tf_op jit(solution)/shard_map/ppermute | solution.py:399
  4.2 0.0 copy-start.1
  4.2 1.7 %take_rest.1 = (f32[2,4,8,2048]{3,2,1,0:T(8,128)S(1)}, f32[2,2,16,2048]{3,2,1,0:T(8,128)S(1)}, f32[2,2,16,2048]{3,2,1,0:T(8,128)S(1)}) custom-call(s32[1]{0:T(128)} %bitcast.7.lat_ref, s32[1]{0:T(128)} %bitcast.depth_ref, f32[16,16,2048]{2,1,0:T(8,128)} %grade_hbm.3, f32[16,16,2048]{2,1,0:T(8,128)} %amp_hbm.3, f32[2,4,8,2048]{3,2,1,0:T(8,128)S(1)} %take_pair.1.after_ref), custom_call_target="tpu_custom_call" | custom-call | tf_op jit(solution)/shard_map/take_rest/pallas_call | solution.py:440
  5.9 0.0 copy-start
  5.9 0.0 copy-start.2
  5.9 0.0 copy-start.3
  5.9 0.8 %collective-permute-start.5 = (f32[2,4,8,2048]{3,2,1,0:T(8,128)S(1)}, f32[2,4,8,2048]{3,2,1,0:T(8,128)S(1)}, u32[]{:S(2)}, u32[]{:S(2)}) collective-permute-start(f32[2,4,8,2048]{3,2,1,0:T(8,128)S(1)} %get-tuple-element.21.refs_1_), channel_id=1, source_target_pairs={{4,8},{8,4},{12,16},{16,12},{20,24},{24,20},{5,9},{9,5},{13,17},{1... | collective-permute-start | bytes 1572872 | tf_op jit(solution)/shard_map/ppermute | solution.py:404
  6.8 0.7 %collective-permute-start.1 = (f32[2,2,16,2048]{3,2,1,0:T(8,128)S(1)}, f32[2,2,16,2048]{3,2,1,0:T(8,128)S(1)}, u32[]{:S(2)}, u32[]{:S(2)}) collective-permute-start(f32[2,2,16,2048]{3,2,1,0:T(8,128)S(1)} %pass_on.2.refs_1_), channel_id=1, source_target_pairs={{1,2},{2,1},{5,6},{6,5},{9,10},{10,9},{13,14},{14,13},{17,18},{18,... | collective-permute-start | bytes 1572872 | tf_op jit(solution)/shard_map/ppermute | solution.py:404
  7.5 2.9 %collective-permute-start = (f32[2,2,16,2048]{3,2,1,0:T(8,128)S(1)}, f32[2,2,16,2048]{3,2,1,0:T(8,128)S(1)}, u32[]{:S(2)}, u32[]{:S(2)}) collective-permute-start(f32[2,2,16,2048]{3,2,1,0:T(8,128)S(1)} %pass_on.3), channel_id=1, source_target_pairs={{0,1},{1,0},{2,3},{3,2},{4,5},{5,4},{6,7},{7,6},{8,9},{9,8},{10,11... | collective-permute-start | bytes 1572872 | tf_op jit(solution)/shard_map/ppermute | solution.py:399
  10.4 0.0 copy-done.1
  10.4 0.0 copy-done
  10.4 0.0 copy-done.2
  10.4 0.0 copy-done.3
  10.4 4.8 %middle.1 = (f32[2,16,4,8,128]{4,3,2,1,0:T(8,128)S(1)}, f32[8,16,9,8,128]{4,3,2,1,0:T(8,128)S(1)}) custom-call(s32[2,2,8]{2,1,0:T(2,128)S(1)} %copy-done.2, f32[4096,128]{1,0:T(8,128)S(1)} %bitcast.22, f32[4096,128]{1,0:T(8,128)S(1)} %bitcast.25, s32[4,128]{1,0:T(4,128)S(1)} %copy-done.3), custom_call_target="tpu_custom_call" | custom-call | flops 10000000000 | bytes 100000000 | tf_op jit(solution)/shard_map/middle/pallas_call | solution.py:461
  15.1 0.0 collective-permute-done
  15.1 0.0 collective-permute-done.1
  15.1 2.5 %ends.2 = (f32[2,4,16,512]{3,2,1,0:T(8,128)S(1)}, f32[4,16,9,8,128]{4,3,2,1,0:T(8,128)S(1)}) custom-call(s32[2,2,8]{2,1,0:T(2,128)S(1)} %copy-done.2, s32[1]{0:T(128)} %bitcast.depth_ref, f32[4096,128]{1,0:T(8,128)S(1)} %bitcast.23, f32[4096,128]{1,0:T(8,128)S(1)} %bitcast.26, f32[1024,128]{1,0:T(8,128)S(1)} %bitcast.30, f32[1024,128]{1,0:T(8,128)S(1)} %bitcast.28, ...), custom_call_target="tpu_custom_call" | custom-call | tf_op jit(solution)/shard_map/ends/pallas_call | solution.py:476
  17.7 2.0 %collective-permute-start.2 = (f32[2,4,16,512]{3,2,1,0:T(8,128)S(1)}, f32[2,4,16,512]{3,2,1,0:T(8,128)S(1)}, u32[]{:S(2)}, u32[]{:S(2)}) collective-permute-start(f32[2,4,16,512]{3,2,1,0:T(8,128)S(1)} %get-tuple-element.24.rest_0_), channel_id=1, source_target_pairs={{0,1},{1,0},{2,3},{3,2},{4,5},{5,4},{6,7},{7,6},{8,9},{9,8},{10,11... | collective-permute-start | bytes 786440 | tf_op jit(solution)/shard_map/ppermute | solution.py:399
  19.7 2.5 %ends.3 = (f32[2,4,16,512]{3,2,1,0:T(8,128)S(1)}, f32[4,16,9,8,128]{4,3,2,1,0:T(8,128)S(1)}) custom-call(s32[2,2,8]{2,1,0:T(2,128)S(1)} %copy-done.2, s32[1]{0:T(128)} %bitcast.depth_ref, f32[4096,128]{1,0:T(8,128)S(1)} %bitcast.24, f32[4096,128]{1,0:T(8,128)S(1)} %bitcast.27, f32[1024,128]{1,0:T(8,128)S(1)} %bitcast.31, f32[1024,128]{1,0:T(8,128)S(1)} %bitcast.29, ...), custom_call_target="tpu_custom_call" | custom-call | tf_op jit(solution)/shard_map/ends/pallas_call | solution.py:476
  22.3 0.0 collective-permute-done.2.got_ref
  22.3 1.7 %collective-permute-start.3 = (f32[4,16,512]{2,1,0:T(8,128)S(1)}, f32[4,16,512]{2,1,0:T(8,128)S(1)}, u32[]{:S(2)}, u32[]{:S(2)}) collective-permute-start(f32[4,16,512]{2,1,0:T(8,128)S(1)} %get-tuple-element.27.after_ref), channel_id=1, source_target_pairs={{0,2},{1,3},{2,0},{3,1},{4,6},{5,7},{6,4},{7,5},{8,10},{9,11},{10,... | collective-permute-start | bytes 393224 | tf_op jit(solution)/shard_map/ppermute | solution.py:490
  24.0 0.0 collective-permute-done.5.cross_ref
  24.0 2.5 %collective-permute-done.4.pair_ref = f32[2,4,8,2048]{3,2,1,0:T(8,128)S(1)} collective-permute-done((f32[2,4,8,2048]{3,2,1,0:T(8,128)S(1)}, f32[2,4,8,2048]{3,2,1,0:T(8,128)S(1)}, u32[]{:S(2)}, u32[]{:S(2)}) %collective-permute-start.4) | collective-permute-done | bytes 524320 | tf_op jit(solution)/shard_map/ppermute | solution.py:399
  26.6 0.5 %edges.2 = (f32[4,8,256]{2,1,0:T(8,128)S(1)}, f32[4,8,256]{2,1,0:T(8,128)S(1)}, f32[4,8,256]{2,1,0:T(8,128)S(1)}) custom-call(s32[1]{0:T(128)} %bitcast.depth_ref, s32[1]{0:T(128)} %bitcast.7.lat_ref, f32[8,16,9,8,128]{4,3,2,1,0:T(8,128)S(1)} %get-tuple-element.23.middle_kept_ref.kept_ref, f32[4,16,9,8,128]{4,3,2,1,0:T(8,128)S(1)} %get-tuple-element.28.stay_ref, ...), custom_call_target="tpu_custom_call" | custom-call | tf_op jit(solution)/shard_map/edges/pallas_call | solution.py:504
  27.1 1.6 %collective-permute-start.6 = (f32[4,8,256]{2,1,0:T(8,128)S(1)}, f32[4,8,256]{2,1,0:T(8,128)S(1)}, u32[]{:S(2)}, u32[]{:S(2)}) collective-permute-start(f32[4,8,256]{2,1,0:T(8,128)S(1)} %get-tuple-element.31), channel_id=1, source_target_pairs={{0,2},{1,3},{2,0},{3,1},{4,6},{5,7},{6,4},{7,5},{8,10},{9,11},{10,... | collective-permute-start | bytes 98312 | tf_op jit(solution)/shard_map/ppermute | solution.py:490
  28.7 0.0 collective-permute-start.7
  28.7 0.6 %collective-permute-start.8 = (f32[4,8,256]{2,1,0:T(8,128)S(1)}, f32[4,8,256]{2,1,0:T(8,128)S(1)}, u32[]{:S(2)}, u32[]{:S(2)}) collective-permute-start(f32[4,8,256]{2,1,0:T(8,128)S(1)} %get-tuple-element.30.after_ref), channel_id=1, source_target_pairs={{0,1},{1,0},{2,3},{3,2},{4,5},{5,4},{6,7},{7,6},{8,9},{9,8},{10,11... | collective-permute-start | bytes 98312 | tf_op jit(solution)/shard_map/ppermute | solution.py:399
  29.3 0.2 edges.3.home_ref
  29.5 1.6 %collective-permute-done.6.across_ref = f32[4,8,256]{2,1,0:T(8,128)S(1)} collective-permute-done((f32[4,8,256]{2,1,0:T(8,128)S(1)}, f32[4,8,256]{2,1,0:T(8,128)S(1)}, u32[]{:S(2)}, u32[]{:S(2)}) %collective-permute-start.6) | collective-permute-done | bytes 32800 | tf_op jit(solution)/shard_map/ppermute | solution.py:490
  31.1 0.9 %collective-permute-done.7.corner_ref = f32[4,8,256]{2,1,0:T(8,128)S(1)} collective-permute-done((f32[4,8,256]{2,1,0:T(8,128)S(1)}, f32[4,8,256]{2,1,0:T(8,128)S(1)}, u32[]{:S(2)}, u32[]{:S(2)}) %collective-permute-start.7) | collective-permute-done | bytes 32800 | tf_op jit(solution)/shard_map/ppermute | solution.py:517
  32.0 0.0 collective-permute-done.8.beside_ref
  32.0 0.0 collective-permute-done.3.got_ref
  32.0 0.7 %finish.1 = f32[4,16,512]{2,1,0:T(8,128)} custom-call(s32[1]{0:T(128)} %bitcast.depth_ref, f32[4,16,512]{2,1,0:T(8,128)S(1)} %get-tuple-element.26.own_ref, f32[4,16,512]{2,1,0:T(8,128)S(1)} %collective-permute-done.3.got_ref, f32[4,8,256]{2,1,0:T(8,128)S(1)} %edges.3.home_ref, f32[4,8,256]{2,1,0:T(8,128)S(1)} %collective-permute-done.6.across_ref, ...), custom_call_target="tpu_custom_call" | custom-call | tf_op jit(solution)/shard_map/finish/pallas_call | solution.py:519
  (3 shorter events, 0.0 us)
Async XLA Ops:
  1.1 25.4 %collective-permute-start.4 = (f32[2,4,8,2048]{3,2,1,0:T(8,128)S(1)}, f32[2,4,8,2048]{3,2,1,0:T(8,128)S(1)}, u32[]{:S(2)}, u32[]{:S(2)}) collective-permute-start(f32[2,4,8,2048]{3,2,1,0:T(8,128)S(1)} %take_pair.1.after_ref), channel_id=1, source_target_pairs={{0,4},{4,0},{8,12},{12,8},{16,20},{20,16},{24,28},{28,24},{1,5},{5... | collective-permute-start | bytes 1572872 | tf_op jit(solution)/shard_map/ppermute | solution.py:399
  4.2 6.2 %copy-start.1 = (f32[16,16,2048]{2,1,0:T(8,128)S(1)}, f32[16,16,2048]{2,1,0:T(8,128)}, u32[]{:S(2)}) copy-start(f32[16,16,2048]{2,1,0:T(8,128)} %amp_hbm.3) | copy-start | bytes 6291460
  5.9 4.5 %copy-start = (f32[16,16,2048]{2,1,0:T(8,128)S(1)}, f32[16,16,2048]{2,1,0:T(8,128)}, u32[]{:S(2)}) copy-start(f32[16,16,2048]{2,1,0:T(8,128)} %grade_hbm.3) | copy-start | bytes 6291460
  5.9 4.5 %copy-start.2 = (s32[2,2,8]{2,1,0:T(2,128)S(1)}, s32[2,2,8]{2,1,0:T(2,128)}, u32[]{:S(2)}) copy-start(s32[2,2,8]{2,1,0:T(2,128)} %mask_ref.5) | copy-start | bytes 388
  5.9 4.5 %copy-start.3 = (s32[4,128]{1,0:T(4,128)S(1)}, s32[4,128]{1,0:T(4,128)}, u32[]{:S(2)}) copy-start(s32[4,128]{1,0:T(4,128)} %table_ref.5) | copy-start | bytes 6148
  5.9 18.1 %collective-permute-start.5 = (f32[2,4,8,2048]{3,2,1,0:T(8,128)S(1)}, f32[2,4,8,2048]{3,2,1,0:T(8,128)S(1)}, u32[]{:S(2)}, u32[]{:S(2)}) collective-permute-start(f32[2,4,8,2048]{3,2,1,0:T(8,128)S(1)} %get-tuple-element.21.refs_1_), channel_id=1, source_target_pairs={{4,8},{8,4},{12,16},{16,12},{20,24},{24,20},{5,9},{9,5},{13,17},{1... | collective-permute-start | bytes 1572872 | tf_op jit(solution)/shard_map/ppermute | solution.py:404
  6.8 8.4 %collective-permute-start.1 = (f32[2,2,16,2048]{3,2,1,0:T(8,128)S(1)}, f32[2,2,16,2048]{3,2,1,0:T(8,128)S(1)}, u32[]{:S(2)}, u32[]{:S(2)}) collective-permute-start(f32[2,2,16,2048]{3,2,1,0:T(8,128)S(1)} %pass_on.2.refs_1_), channel_id=1, source_target_pairs={{1,2},{2,1},{5,6},{6,5},{9,10},{10,9},{13,14},{14,13},{17,18},{18,... | collective-permute-start | bytes 1572872 | tf_op jit(solution)/shard_map/ppermute | solution.py:404
  7.5 7.7 %collective-permute-start = (f32[2,2,16,2048]{3,2,1,0:T(8,128)S(1)}, f32[2,2,16,2048]{3,2,1,0:T(8,128)S(1)}, u32[]{:S(2)}, u32[]{:S(2)}) collective-permute-start(f32[2,2,16,2048]{3,2,1,0:T(8,128)S(1)} %pass_on.3), channel_id=1, source_target_pairs={{0,1},{1,0},{2,3},{3,2},{4,5},{5,4},{6,7},{7,6},{8,9},{9,8},{10,11... | collective-permute-start | bytes 1572872 | tf_op jit(solution)/shard_map/ppermute | solution.py:399
  17.7 4.6 %collective-permute-start.2 = (f32[2,4,16,512]{3,2,1,0:T(8,128)S(1)}, f32[2,4,16,512]{3,2,1,0:T(8,128)S(1)}, u32[]{:S(2)}, u32[]{:S(2)}) collective-permute-start(f32[2,4,16,512]{3,2,1,0:T(8,128)S(1)} %get-tuple-element.24.rest_0_), channel_id=1, source_target_pairs={{0,1},{1,0},{2,3},{3,2},{4,5},{5,4},{6,7},{7,6},{8,9},{9,8},{10,11... | collective-permute-start | bytes 786440 | tf_op jit(solution)/shard_map/ppermute | solution.py:399
  22.3 9.7 %collective-permute-start.3 = (f32[4,16,512]{2,1,0:T(8,128)S(1)}, f32[4,16,512]{2,1,0:T(8,128)S(1)}, u32[]{:S(2)}, u32[]{:S(2)}) collective-permute-start(f32[4,16,512]{2,1,0:T(8,128)S(1)} %get-tuple-element.27.after_ref), channel_id=1, source_target_pairs={{0,2},{1,3},{2,0},{3,1},{4,6},{5,7},{6,4},{7,5},{8,10},{9,11},{10,... | collective-permute-start | bytes 393224 | tf_op jit(solution)/shard_map/ppermute | solution.py:490
  27.1 4.0 %collective-permute-start.6 = (f32[4,8,256]{2,1,0:T(8,128)S(1)}, f32[4,8,256]{2,1,0:T(8,128)S(1)}, u32[]{:S(2)}, u32[]{:S(2)}) collective-permute-start(f32[4,8,256]{2,1,0:T(8,128)S(1)} %get-tuple-element.31), channel_id=1, source_target_pairs={{0,2},{1,3},{2,0},{3,1},{4,6},{5,7},{6,4},{7,5},{8,10},{9,11},{10,... | collective-permute-start | bytes 98312 | tf_op jit(solution)/shard_map/ppermute | solution.py:490
  28.7 3.3 %collective-permute-start.7 = (f32[4,8,256]{2,1,0:T(8,128)S(1)}, f32[4,8,256]{2,1,0:T(8,128)S(1)}, u32[]{:S(2)}, u32[]{:S(2)}) collective-permute-start(f32[4,8,256]{2,1,0:T(8,128)S(1)} %get-tuple-element.32), channel_id=1, source_target_pairs={{0,3},{1,2},{2,1},{3,0},{4,7},{5,6},{6,5},{7,4},{8,11},{9,10},{10,... | collective-permute-start | bytes 98312 | tf_op jit(solution)/shard_map/ppermute | solution.py:517
  28.7 3.3 %collective-permute-start.8 = (f32[4,8,256]{2,1,0:T(8,128)S(1)}, f32[4,8,256]{2,1,0:T(8,128)S(1)}, u32[]{:S(2)}, u32[]{:S(2)}) collective-permute-start(f32[4,8,256]{2,1,0:T(8,128)S(1)} %get-tuple-element.30.after_ref), channel_id=1, source_target_pairs={{0,1},{1,0},{2,3},{3,2},{4,5},{5,4},{6,7},{7,6},{8,9},{9,8},{10,11... | collective-permute-start | bytes 98312 | tf_op jit(solution)/shard_map/ppermute | solution.py:399
where the time goes:
time: 32.9 us; the launch traced here: 32.7 us
  Pallas kernels  14.1 us (43%)
  starting transfers between devices  13.4 us (41%)
  waiting for transfers between devices  5.07 us (15%)
    ppermute x4, starting transfers between devices, swap_near(): lax.ppermute(x, axis, [(i, i ^ 1) for i in range(lax.axis_size(axis))])  8.61 us
    pallas_call x2, Pallas kernels, march_ends(): pl.pallas_call(functools.partial(ends_kernel, scale, pieces, slices, stri...  5.07 us
    pallas_call x1, Pallas kernels, local(): pl.pallas_call(functools.partial(middle_kernel, scale, slices, strips), o...  4.75 us
    ppermute x2, starting transfers between devices, swap_across(): return lax.ppermute(x, 'depth', [(i, i ^ 2) for i in range(pieces)])  3.26 us
    ppermute x4, waiting for transfers between devices, swap_near(): lax.ppermute(x, axis, [(i, i ^ 1) for i in range(lax.axis_size(axis))])  2.56 us
    pallas_call x1, Pallas kernels, local(): pl.pallas_call(rest_kernel, out_shape=(lat_halo, depth_halo, depth_halo),...  1.69 us
    ppermute x2, waiting for transfers between devices, swap_across(): return lax.ppermute(x, 'depth', [(i, i ^ 2) for i in range(pieces)])  1.59 us
    ppermute x2, starting transfers between devices, swap_far(): lax.ppermute(x, axis, [(i, j) for k in range(1, size - 1, 2) for i, j in...  1.52 us
  transfers between devices with their start and end apart: 9, of which 3 were waited for; matrix products, arithmetic and copies ran while one was open for 0% of the time, Pallas kernels for 38%

commit v1 on v0

--- a/solution.py
+++ b/solution.py
@@ -202,22 +202,23 @@
     def block(cb, carry):
         for rt in range(2):
             def march(halves):
-                for j in range(per_block):
-                    s = cb * per_block + j
-                    fields = [Field(ref, slices, strips, s) for ref in (grade_ref, amp_ref)]
-                    state = (zero, zero, zero, zero + 1.0)
-                    for zb in halves:
-                        for zi in range(2 - 2 * zb, MZ - 2 * zb):
-                            z = zb * MZ + zi
-                            along = [[field.load(z + k, rt) for k in (-2, -1, 1, 2)] for field in fields]
-                            terms = cell_terms(fields, z, rt, along, False, bins, low_ref, high_ref)
+                tiles = [cb * per_block + j for j in range(per_block)]
+                fields = [[Field(ref, slices, strips, s) for ref in (grade_ref, amp_ref)] for s in tiles]
+                states = [(zero, zero, zero, zero + 1.0)] * per_block
+                for zb in halves:
+                    for zi in range(2 - 2 * zb, MZ - 2 * zb):
+                        z = zb * MZ + zi
+                        for j, s in enumerate(tiles):
+                            along = [[field.load(z + k, rt) for k in (-2, -1, 1, 2)] for field in fields[j]]
+                            terms = cell_terms(fields[j], z, rt, along, False, bins, low_ref, high_ref)
                             keep(kept_ref, zi, s, rt, zb, terms)
-                            state = step(state, terms)
+                            states[j] = step(states[j], terms)
+                for j, s in enumerate(tiles):
                     for zb in {0, 1} - set(halves):
                         for zi in range(2 - 2 * zb, MZ - 2 * zb):
                             blank(kept_ref, zi, s, rt, zb)
                     for c in range(4):
-                        mid_ref[rt, s, c] = state[c]
+                        mid_ref[rt, s, c] = states[j][c]
 
             front, back = mask_ref[0, rt, cb] != 0, mask_ref[1, rt, cb] != 0
             pl.when(front & back)(functools.partial(march, (0, 1)))

time: 32.9 us -> 32.9 us (level)
  starting transfers between devices: 13.4 us -> 11.6 us
  Pallas kernels: 14.1 us -> 15.5 us
  waiting for transfers between devices: 5.07 us -> 5.48 us
    pallas_call x1, Pallas kernels: 4.75 us -> 6.18 us  [local(): pl.pallas_call(functools.partial(middle_kernel, scale, slices, strips), o...]
    ppermute x4, starting transfers between devices: 8.61 us -> 7.48 us  [swap_near(): lax.ppermute(x, axis, [(i, i ^ 1) for i in range(lax.axis_size(axis))])]
    ppermute x2, starting transfers between devices: 3.26 us -> 2.55 us  [swap_across(): return lax.ppermute(x, 'depth', [(i, i ^ 2) for i in range(pieces)])]
    ppermute x4, waiting for transfers between devices: 2.56 us -> 2.97 us  [swap_near(): lax.ppermute(x, axis, [(i, i ^ 1) for i in range(lax.axis_size(axis))])]
  transfers between devices with their start and end apart: 9 -> 9, of which waited for: 3 -> 3; matrix products, arithmetic and copies ran while one was open for 0% -> 0% of each run, Pallas kernels for 38% -> 42%
where the time goes in v1:
time: 32.9 us; the launch traced here: 32.7 us
  Pallas kernels  15.5 us (47%)
  starting transfers between devices  11.6 us (35%)
  waiting for transfers between devices  5.48 us (17%)
    ppermute x4, starting transfers between devices, swap_near(): lax.ppermute(x, axis, [(i, i ^ 1) for i in range(lax.axis_size(axis))])  7.48 us
    pallas_call x1, Pallas kernels, local(): pl.pallas_call(functools.partial(middle_kernel, scale, slices, strips), o...  6.18 us
    pallas_call x2, Pallas kernels, march_ends(): pl.pallas_call(functools.partial(ends_kernel, scale, pieces, slices, stri...  5.07 us
    ppermute x4, waiting for transfers between devices, swap_near(): lax.ppermute(x, axis, [(i, i ^ 1) for i in range(lax.axis_size(axis))])  2.97 us
    ppermute x2, starting transfers between devices, swap_across(): return lax.ppermute(x, 'depth', [(i, i ^ 2) for i in range(pieces)])  2.55 us
    pallas_call x1, Pallas kernels, local(): pl.pallas_call(rest_kernel, out_shape=(lat_halo, depth_halo, depth_halo),...  1.69 us
    ppermute x2, waiting for transfers between devices, swap_across(): return lax.ppermute(x, 'depth', [(i, i ^ 2) for i in range(pieces)])  1.59 us
    ppermute x2, starting transfers between devices, swap_far(): lax.ppermute(x, axis, [(i, j) for k in range(1, size - 1, 2) for i, j in...  1.52 us
  transfers between devices with their start and end apart: 9, of which 3 were waited for; matrix products, arithmetic and copies ran while one was open for 0% of the time, Pallas kernels for 42%

profile of v1, /device:TPU:0, one launch (start us, length us, event | category | flops | bytes accessed | tf_op | source)
XLA Modules:
  0.0 32.7 jit_solution(13306680890740113142)
XLA Ops:
  0.0 1.1 %take_pair.1.after_ref = f32[2,4,8,2048]{3,2,1,0:T(8,128)S(1)} custom-call(s32[1]{0:T(128)} %bitcast.7.lat_ref, f32[16,16,2048]{2,1,0:T(8,128)} %grade_hbm.3, f32[16,16,2048]{2,1,0:T(8,128)} %amp_hbm.3), custom_call_target="tpu_custom_call" | custom-call | tf_op jit(solution)/shard_map/take_pair/pallas_call | solution.py:432
  1.1 3.0 %collective-permute-start.4 = (f32[2,4,8,2048]{3,2,1,0:T(8,128)S(1)}, f32[2,4,8,2048]{3,2,1,0:T(8,128)S(1)}, u32[]{:S(2)}, u32[]{:S(2)}) collective-permute-start(f32[2,4,8,2048]{3,2,1,0:T(8,128)S(1)} %take_pair.1.after_ref), channel_id=1, source_target_pairs={{0,4},{4,0},{8,12},{12,8},{16,20},{20,16},{24,28},{28,24},{1,5},{5... | collective-permute-start | bytes 1572872 | tf_op jit(solution)/shard_map/ppermute | solution.py:400
  4.2 0.0 copy-start.1
  4.2 1.7 %take_rest.1 = (f32[2,4,8,2048]{3,2,1,0:T(8,128)S(1)}, f32[2,2,16,2048]{3,2,1,0:T(8,128)S(1)}, f32[2,2,16,2048]{3,2,1,0:T(8,128)S(1)}) custom-call(s32[1]{0:T(128)} %bitcast.7.lat_ref, s32[1]{0:T(128)} %bitcast.depth_ref, f32[16,16,2048]{2,1,0:T(8,128)} %grade_hbm.3, f32[16,16,2048]{2,1,0:T(8,128)} %amp_hbm.3, f32[2,4,8,2048]{3,2,1,0:T(8,128)S(1)} %take_pair.1.after_ref), custom_call_target="tpu_custom_call" | custom-call | tf_op jit(solution)/shard_map/take_rest/pallas_call | solution.py:441
  5.9 0.0 copy-start
  5.9 0.0 copy-start.2
  5.9 0.0 copy-start.3
  5.9 0.8 %collective-permute-start.5 = (f32[2,4,8,2048]{3,2,1,0:T(8,128)S(1)}, f32[2,4,8,2048]{3,2,1,0:T(8,128)S(1)}, u32[]{:S(2)}, u32[]{:S(2)}) collective-permute-start(f32[2,4,8,2048]{3,2,1,0:T(8,128)S(1)} %get-tuple-element.21.refs_1_), channel_id=1, source_target_pairs={{4,8},{8,4},{12,16},{16,12},{20,24},{24,20},{5,9},{9,5},{13,17},{1... | collective-permute-start | bytes 1572872 | tf_op jit(solution)/shard_map/ppermute | solution.py:405
  6.8 0.7 %collective-permute-start.1 = (f32[2,2,16,2048]{3,2,1,0:T(8,128)S(1)}, f32[2,2,16,2048]{3,2,1,0:T(8,128)S(1)}, u32[]{:S(2)}, u32[]{:S(2)}) collective-permute-start(f32[2,2,16,2048]{3,2,1,0:T(8,128)S(1)} %pass_on.2.refs_1_), channel_id=1, source_target_pairs={{1,2},{2,1},{5,6},{6,5},{9,10},{10,9},{13,14},{14,13},{17,18},{18,... | collective-permute-start | bytes 1572872 | tf_op jit(solution)/shard_map/ppermute | solution.py:405
  7.5 2.9 %collective-permute-start = (f32[2,2,16,2048]{3,2,1,0:T(8,128)S(1)}, f32[2,2,16,2048]{3,2,1,0:T(8,128)S(1)}, u32[]{:S(2)}, u32[]{:S(2)}) collective-permute-start(f32[2,2,16,2048]{3,2,1,0:T(8,128)S(1)} %pass_on.3), channel_id=1, source_target_pairs={{0,1},{1,0},{2,3},{3,2},{4,5},{5,4},{6,7},{7,6},{8,9},{9,8},{10,11... | collective-permute-start | bytes 1572872 | tf_op jit(solution)/shard_map/ppermute | solution.py:400
  10.4 0.0 copy-done.1
  10.4 0.0 copy-done
  10.4 0.0 copy-done.2
  10.4 0.0 copy-done.3
  10.4 6.2 %middle.1 = (f32[2,16,4,8,128]{4,3,2,1,0:T(8,128)S(1)}, f32[8,16,9,8,128]{4,3,2,1,0:T(8,128)S(1)}) custom-call(s32[2,2,8]{2,1,0:T(2,128)S(1)} %copy-done.2, f32[4096,128]{1,0:T(8,128)S(1)} %bitcast.22, f32[4096,128]{1,0:T(8,128)S(1)} %bitcast.25, s32[4,128]{1,0:T(4,128)S(1)} %copy-done.3), custom_call_target="tpu_custom_call" | custom-call | flops 10000000000 | bytes 100000000 | tf_op jit(solution)/shard_map/middle/pallas_call | solution.py:462
  16.6 0.0 collective-permute-done
  16.6 0.0 collective-permute-done.1
  16.6 2.5 %ends.2 = (f32[2,4,16,512]{3,2,1,0:T(8,128)S(1)}, f32[4,16,9,8,128]{4,3,2,1,0:T(8,128)S(1)}) custom-call(s32[2,2,8]{2,1,0:T(2,128)S(1)} %copy-done.2, s32[1]{0:T(128)} %bitcast.depth_ref, f32[4096,128]{1,0:T(8,128)S(1)} %bitcast.23, f32[4096,128]{1,0:T(8,128)S(1)} %bitcast.26, f32[1024,128]{1,0:T(8,128)S(1)} %bitcast.30, f32[1024,128]{1,0:T(8,128)S(1)} %bitcast.28, ...), custom_call_target="tpu_custom_call" | custom-call | tf_op jit(solution)/shard_map/ends/pallas_call | solution.py:477
  19.1 0.9 %collective-permute-start.2 = (f32[2,4,16,512]{3,2,1,0:T(8,128)S(1)}, f32[2,4,16,512]{3,2,1,0:T(8,128)S(1)}, u32[]{:S(2)}, u32[]{:S(2)}) collective-permute-start(f32[2,4,16,512]{3,2,1,0:T(8,128)S(1)} %get-tuple-element.24.rest_0_), channel_id=1, source_target_pairs={{0,1},{1,0},{2,3},{3,2},{4,5},{5,4},{6,7},{7,6},{8,9},{9,8},{10,11... | collective-permute-start | bytes 786440 | tf_op jit(solution)/shard_map/ppermute | solution.py:400
  20.0 2.5 %ends.3 = (f32[2,4,16,512]{3,2,1,0:T(8,128)S(1)}, f32[4,16,9,8,128]{4,3,2,1,0:T(8,128)S(1)}) custom-call(s32[2,2,8]{2,1,0:T(2,128)S(1)} %copy-done.2, s32[1]{0:T(128)} %bitcast.depth_ref, f32[4096,128]{1,0:T(8,128)S(1)} %bitcast.24, f32[4096,128]{1,0:T(8,128)S(1)} %bitcast.27, f32[1024,128]{1,0:T(8,128)S(1)} %bitcast.31, f32[1024,128]{1,0:T(8,128)S(1)} %bitcast.29, ...), custom_call_target="tpu_custom_call" | custom-call | tf_op jit(solution)/shard_map/ends/pallas_call | solution.py:477
  22.6 0.0 collective-permute-done.2.got_ref
  22.6 1.0 %collective-permute-start.3 = (f32[4,16,512]{2,1,0:T(8,128)S(1)}, f32[4,16,512]{2,1,0:T(8,128)S(1)}, u32[]{:S(2)}, u32[]{:S(2)}) collective-permute-start(f32[4,16,512]{2,1,0:T(8,128)S(1)} %get-tuple-element.27.after_ref), channel_id=1, source_target_pairs={{0,2},{1,3},{2,0},{3,1},{4,6},{5,7},{6,4},{7,5},{8,10},{9,11},{10,... | collective-permute-start | bytes 393224 | tf_op jit(solution)/shard_map/ppermute | solution.py:491
  23.6 0.0 collective-permute-done.5.cross_ref
  23.6 3.0 %collective-permute-done.4.pair_ref = f32[2,4,8,2048]{3,2,1,0:T(8,128)S(1)} collective-permute-done((f32[2,4,8,2048]{3,2,1,0:T(8,128)S(1)}, f32[2,4,8,2048]{3,2,1,0:T(8,128)S(1)}, u32[]{:S(2)}, u32[]{:S(2)}) %collective-permute-start.4) | collective-permute-done | bytes 524320 | tf_op jit(solution)/shard_map/ppermute | solution.py:400
  26.6 0.5 %edges.2 = (f32[4,8,256]{2,1,0:T(8,128)S(1)}, f32[4,8,256]{2,1,0:T(8,128)S(1)}, f32[4,8,256]{2,1,0:T(8,128)S(1)}) custom-call(s32[1]{0:T(128)} %bitcast.depth_ref, s32[1]{0:T(128)} %bitcast.7.lat_ref, f32[8,16,9,8,128]{4,3,2,1,0:T(8,128)S(1)} %get-tuple-element.23.middle_kept_ref.kept_ref, f32[4,16,9,8,128]{4,3,2,1,0:T(8,128)S(1)} %get-tuple-element.28.stay_ref, ...), custom_call_target="tpu_custom_call" | custom-call | tf_op jit(solution)/shard_map/edges/pallas_call | solution.py:505
  27.1 1.6 %collective-permute-start.6 = (f32[4,8,256]{2,1,0:T(8,128)S(1)}, f32[4,8,256]{2,1,0:T(8,128)S(1)}, u32[]{:S(2)}, u32[]{:S(2)}) collective-permute-start(f32[4,8,256]{2,1,0:T(8,128)S(1)} %get-tuple-element.31), channel_id=1, source_target_pairs={{0,2},{1,3},{2,0},{3,1},{4,6},{5,7},{6,4},{7,5},{8,10},{9,11},{10,... | collective-permute-start | bytes 98312 | tf_op jit(solution)/shard_map/ppermute | solution.py:491
  28.7 0.0 collective-permute-start.7
  28.7 0.6 %collective-permute-start.8 = (f32[4,8,256]{2,1,0:T(8,128)S(1)}, f32[4,8,256]{2,1,0:T(8,128)S(1)}, u32[]{:S(2)}, u32[]{:S(2)}) collective-permute-start(f32[4,8,256]{2,1,0:T(8,128)S(1)} %get-tuple-element.30.after_ref), channel_id=1, source_target_pairs={{0,1},{1,0},{2,3},{3,2},{4,5},{5,4},{6,7},{7,6},{8,9},{9,8},{10,11... | collective-permute-start | bytes 98312 | tf_op jit(solution)/shard_map/ppermute | solution.py:400
  29.3 0.2 edges.3.home_ref
  29.5 1.6 %collective-permute-done.6.across_ref = f32[4,8,256]{2,1,0:T(8,128)S(1)} collective-permute-done((f32[4,8,256]{2,1,0:T(8,128)S(1)}, f32[4,8,256]{2,1,0:T(8,128)S(1)}, u32[]{:S(2)}, u32[]{:S(2)}) %collective-permute-start.6) | collective-permute-done | bytes 32800 | tf_op jit(solution)/shard_map/ppermute | solution.py:491
  31.1 0.9 %collective-permute-done.7.corner_ref = f32[4,8,256]{2,1,0:T(8,128)S(1)} collective-permute-done((f32[4,8,256]{2,1,0:T(8,128)S(1)}, f32[4,8,256]{2,1,0:T(8,128)S(1)}, u32[]{:S(2)}, u32[]{:S(2)}) %collective-permute-start.7) | collective-permute-done | bytes 32800 | tf_op jit(solution)/shard_map/ppermute | solution.py:518
  32.0 0.0 collective-permute-done.8.beside_ref
  32.0 0.0 collective-permute-done.3.got_ref
  32.0 0.7 %finish.1 = f32[4,16,512]{2,1,0:T(8,128)} custom-call(s32[1]{0:T(128)} %bitcast.depth_ref, f32[4,16,512]{2,1,0:T(8,128)S(1)} %get-tuple-element.26.own_ref, f32[4,16,512]{2,1,0:T(8,128)S(1)} %collective-permute-done.3.got_ref, f32[4,8,256]{2,1,0:T(8,128)S(1)} %edges.3.home_ref, f32[4,8,256]{2,1,0:T(8,128)S(1)} %collective-permute-done.6.across_ref, ...), custom_call_target="tpu_custom_call" | custom-call | tf_op jit(solution)/shard_map/finish/pallas_call | solution.py:520
  (3 shorter events, 0.0 us)
Async XLA Ops:
  1.1 25.4 %collective-permute-start.4 = (f32[2,4,8,2048]{3,2,1,0:T(8,128)S(1)}, f32[2,4,8,2048]{3,2,1,0:T(8,128)S(1)}, u32[]{:S(2)}, u32[]{:S(2)}) collective-permute-start(f32[2,4,8,2048]{3,2,1,0:T(8,128)S(1)} %take_pair.1.after_ref), channel_id=1, source_target_pairs={{0,4},{4,0},{8,12},{12,8},{16,20},{20,16},{24,28},{28,24},{1,5},{5... | collective-permute-start | bytes 1572872 | tf_op jit(solution)/shard_map/ppermute | solution.py:400
  4.2 6.2 %copy-start.1 = (f32[16,16,2048]{2,1,0:T(8,128)S(1)}, f32[16,16,2048]{2,1,0:T(8,128)}, u32[]{:S(2)}) copy-start(f32[16,16,2048]{2,1,0:T(8,128)} %amp_hbm.3) | copy-start | bytes 6291460
  5.9 4.5 %copy-start = (f32[16,16,2048]{2,1,0:T(8,128)S(1)}, f32[16,16,2048]{2,1,0:T(8,128)}, u32[]{:S(2)}) copy-start(f32[16,16,2048]{2,1,0:T(8,128)} %grade_hbm.3) | copy-start | bytes 6291460
  5.9 4.5 %copy-start.2 = (s32[2,2,8]{2,1,0:T(2,128)S(1)}, s32[2,2,8]{2,1,0:T(2,128)}, u32[]{:S(2)}) copy-start(s32[2,2,8]{2,1,0:T(2,128)} %mask_ref.5) | copy-start | bytes 388
  5.9 4.5 %copy-start.3 = (s32[4,128]{1,0:T(4,128)S(1)}, s32[4,128]{1,0:T(4,128)}, u32[]{:S(2)}) copy-start(s32[4,128]{1,0:T(4,128)} %table_ref.5) | copy-start | bytes 6148
  5.9 17.7 %collective-permute-start.5 = (f32[2,4,8,2048]{3,2,1,0:T(8,128)S(1)}, f32[2,4,8,2048]{3,2,1,0:T(8,128)S(1)}, u32[]{:S(2)}, u32[]{:S(2)}) collective-permute-start(f32[2,4,8,2048]{3,2,1,0:T(8,128)S(1)} %get-tuple-element.21.refs_1_), channel_id=1, source_target_pairs={{4,8},{8,4},{12,16},{16,12},{20,24},{24,20},{5,9},{9,5},{13,17},{1... | collective-permute-start | bytes 1572872 | tf_op jit(solution)/shard_map/ppermute | solution.py:405
  6.8 9.8 %collective-permute-start.1 = (f32[2,2,16,2048]{3,2,1,0:T(8,128)S(1)}, f32[2,2,16,2048]{3,2,1,0:T(8,128)S(1)}, u32[]{:S(2)}, u32[]{:S(2)}) collective-permute-start(f32[2,2,16,2048]{3,2,1,0:T(8,128)S(1)} %pass_on.2.refs_1_), channel_id=1, source_target_pairs={{1,2},{2,1},{5,6},{6,5},{9,10},{10,9},{13,14},{14,13},{17,18},{18,... | collective-permute-start | bytes 1572872 | tf_op jit(solution)/shard_map/ppermute | solution.py:405
  7.5 9.1 %collective-permute-start = (f32[2,2,16,2048]{3,2,1,0:T(8,128)S(1)}, f32[2,2,16,2048]{3,2,1,0:T(8,128)S(1)}, u32[]{:S(2)}, u32[]{:S(2)}) collective-permute-start(f32[2,2,16,2048]{3,2,1,0:T(8,128)S(1)} %pass_on.3), channel_id=1, source_target_pairs={{0,1},{1,0},{2,3},{3,2},{4,5},{5,4},{6,7},{7,6},{8,9},{9,8},{10,11... | collective-permute-start | bytes 1572872 | tf_op jit(solution)/shard_map/ppermute | solution.py:400
  19.1 3.5 %collective-permute-start.2 = (f32[2,4,16,512]{3,2,1,0:T(8,128)S(1)}, f32[2,4,16,512]{3,2,1,0:T(8,128)S(1)}, u32[]{:S(2)}, u32[]{:S(2)}) collective-permute-start(f32[2,4,16,512]{3,2,1,0:T(8,128)S(1)} %get-tuple-element.24.rest_0_), channel_id=1, source_target_pairs={{0,1},{1,0},{2,3},{3,2},{4,5},{5,4},{6,7},{7,6},{8,9},{9,8},{10,11... | collective-permute-start | bytes 786440 | tf_op jit(solution)/shard_map/ppermute | solution.py:400
  22.6 9.4 %collective-permute-start.3 = (f32[4,16,512]{2,1,0:T(8,128)S(1)}, f32[4,16,512]{2,1,0:T(8,128)S(1)}, u32[]{:S(2)}, u32[]{:S(2)}) collective-permute-start(f32[4,16,512]{2,1,0:T(8,128)S(1)} %get-tuple-element.27.after_ref), channel_id=1, source_target_pairs={{0,2},{1,3},{2,0},{3,1},{4,6},{5,7},{6,4},{7,5},{8,10},{9,11},{10,... | collective-permute-start | bytes 393224 | tf_op jit(solution)/shard_map/ppermute | solution.py:491
  27.1 4.0 %collective-permute-start.6 = (f32[4,8,256]{2,1,0:T(8,128)S(1)}, f32[4,8,256]{2,1,0:T(8,128)S(1)}, u32[]{:S(2)}, u32[]{:S(2)}) collective-permute-start(f32[4,8,256]{2,1,0:T(8,128)S(1)} %get-tuple-element.31), channel_id=1, source_target_pairs={{0,2},{1,3},{2,0},{3,1},{4,6},{5,7},{6,4},{7,5},{8,10},{9,11},{10,... | collective-permute-start | bytes 98312 | tf_op jit(solution)/shard_map/ppermute | solution.py:491
  28.7 3.3 %collective-permute-start.7 = (f32[4,8,256]{2,1,0:T(8,128)S(1)}, f32[4,8,256]{2,1,0:T(8,128)S(1)}, u32[]{:S(2)}, u32[]{:S(2)}) collective-permute-start(f32[4,8,256]{2,1,0:T(8,128)S(1)} %get-tuple-element.32), channel_id=1, source_target_pairs={{0,3},{1,2},{2,1},{3,0},{4,7},{5,6},{6,5},{7,4},{8,11},{9,10},{10,... | collective-permute-start | bytes 98312 | tf_op jit(solution)/shard_map/ppermute | solution.py:518
  28.7 3.3 %collective-permute-start.8 = (f32[4,8,256]{2,1,0:T(8,128)S(1)}, f32[4,8,256]{2,1,0:T(8,128)S(1)}, u32[]{:S(2)}, u32[]{:S(2)}) collective-permute-start(f32[4,8,256]{2,1,0:T(8,128)S(1)} %get-tuple-element.30.after_ref), channel_id=1, source_target_pairs={{0,1},{1,0},{2,3},{3,2},{4,5},{5,4},{6,7},{7,6},{8,9},{9,8},{10,11... | collective-permute-start | bytes 98312 | tf_op jit(solution)/shard_map/ppermute | solution.py:400
